TPU v7x, 128 devices: a whole 4x4x4 slice. The times are simulated.
128 devices in a mesh: slab: 16 (over z, y_hi, core), deal: 8 (over x, y_lo).
Axes of the slice: x: 4, y: 4 (y_hi: 2, y_lo: 2; y = y_hi * 2 + y_lo), z: 4, core: 2. Of those that a mesh axis runs over, the one named last changes fastest.
Arguments:
- offsets: float32 [131072, 3, 128], P(('slab', 'deal')), may hold values from -0.5 to 0.5
- velocity: float32 [131072, 3, 128], P(('slab', 'deal')), may hold values from -6 to 6
- affine: float32 [131072, 9, 128], P(('slab', 'deal')), may hold values from -6 to 6
- particle_mass: float32 [131072, 128], P(('slab', 'deal')), may hold values from 0.5 to 2
- cell_in_tile: int32 [131072, 128], P(('slab', 'deal')), may hold values from 0 to 255
- block_tile: int32 [131072], P(('slab', 'deal')), may hold values from 0 to 2047, as said below
- live_blocks: int32 [16, 8], P('slab', 'deal'), may hold values from 512 to 1024, as said below
- send_lists: int32 [16, 8, 2, 16], P('slab', 'deal'), may hold values from 0 to 1023, as said below
- send_counts: int32 [16, 8, 2], P('slab', 'deal'), may hold values from 0 to 16, as said below
Outputs:
- updated_particles: float32 [131072, 15, 128], P(('slab', 'deal'))
- arrivals: float32 [16, 8, 2, 16, 16, 128], P('slab', 'deal')
- grid_velocity: float32 [3, 1024, 8192], P(None, 'slab', 'deal')
Inputs may be any that keep to these rules, and one draw needn't show every extreme that they name: `block_tile`: blocks are sorted by cell: on device (s, d) the tiles never fall along its blocks and lie in [max(d * R - M, 0), min((d + 1) * R + M, 2048)) with R = 256 and M = max(R // 16, 1); some device with d > 0 reaches d * R - M. `live_blocks`: some device has all 1024 blocks live. `send_lists`: the 32 entries of one device's two lists are distinct blocks of that device. `send_counts`: counts toward a slab beyond the ends are zero; some device sends 16 blocks downslope.
All inputs are finite; a program needn't handle non-finite values.
Results may differ from a plain program's by a relative error of at most 0.000073.
Values sent between devices are 32-bit elements; how exact they have to be, the bound alone decides.
No kernel may reach another device: no remote copies, remote signals or barrier semaphores. Data moves between devices by JAX's collectives and lax.ppermute only.
A program may use at most 128 MiB of HBM per device.

v0:
```python
import math
import jax
import jax.numpy as jnp
from jax import lax
from jax.sharding import PartitionSpec as P

PX = 64
PLANE = 8192
TILE = 256
time_step = 0.1
viscosity = 0.2
gravity_pull = (3.0, 0.0, -5.0)


def extended(x, sides, width):
    for axis, dim in sides:
        count, length = (lax.axis_size(axis), x.shape[dim])
        up = [(i, (i + 1) % count) for i in range(count - 1)]
        down = [(j, i) for i, j in up]
        last = lax.slice_in_dim(x, length - width, length, axis=dim)
        initial = lax.slice_in_dim(x, 0, width, axis=dim)
        before = lax.ppermute(last, axis, up)
        after = lax.ppermute(initial, axis, down)
        x = jnp.concatenate([before, x, after], axis=dim)
    return x


def from_behind(x, axis, by):
    count = lax.axis_size(axis)
    pairs = [(i, i + by) for i in range(count) if 0 <= i + by < count]
    return lax.ppermute(x, axis, pairs)


def momentum(offsets, velocity, affine):
    columns = []
    for column in range(3):
        total = velocity[:, column]
        for inner in range(3):
            total = total - affine[:, 3 * column + inner] * offsets[:, inner]
        columns.append(total)
    return jnp.stack(columns, axis=1)


def grid_update(summed):
    floor_mass = jnp.maximum(summed[0], 1.0)
    speeds = []
    for column in range(3):
        speeds.append(summed[1 + column] / floor_mass + time_step * gravity_pull[column])
    return jnp.stack(speeds, axis=0)


def smooth_planes(speed):
    padded = extended(speed, (("slab", 1),), 1)
    return speed + viscosity * (padded[:, 2:] + padded[:, :-2] - 2.0 * speed)


def new_state(offsets, moved):
    shifted = offsets + time_step * moved
    affine_rows = []
    for column in range(3):
        for inner in range(3):
            affine_rows.append(-4.0 * moved[:, column] * offsets[:, inner])
    return jnp.concatenate([shifted, moved, jnp.stack(affine_rows, axis=1)], axis=1)


def body(
    offsets,
    velocity,
    affine,
    particle_mass,
    cell_in_tile,
    block_tile,
    live_blocks,
    send_lists,
    send_counts,
):
    highest = lax.Precision.HIGHEST
    blocks_here = offsets.shape[0]
    deal_count = lax.axis_size("deal")
    deal_index = lax.axis_index("deal")
    tile_count = PX * PLANE // TILE
    active = (jnp.arange(blocks_here, dtype=jnp.int32) < live_blocks[0, 0]).astype(jnp.float32)
    weight = particle_mass * active[:, None]
    moment = momentum(offsets, velocity, affine)
    deposit = jnp.concatenate([weight[:, None, :], weight[:, None, :] * moment], axis=1)
    group_size = math.gcd(blocks_here, 128)
    group_count = blocks_here // group_size
    grouped_deposit = deposit.reshape(group_count, group_size, 4, 128)
    grouped_cells = cell_in_tile.reshape(group_count, group_size, 128)
    grouped_tiles = block_tile.reshape(group_count, group_size)
    tile_slots = jnp.arange(TILE, dtype=jnp.int32)
    tile_labels = jnp.arange(tile_count, dtype=jnp.int32)

    def scatter_group(accumulated, pieces):
        part_deposit, part_cells, part_tiles = pieces
        selector = (part_cells[:, :, None] == tile_slots).astype(jnp.float32)
        per_block = jnp.einsum("bcp,bpk->bck", part_deposit, selector, precision=highest)
        placing = (part_tiles[:, None] == tile_labels).astype(jnp.float32)
        return (
            accumulated + jnp.einsum("bt,bck->ctk", placing, per_block, precision=highest),
            None,
        )

    start_grid = jnp.zeros((4, tile_count, TILE), jnp.float32)
    accumulated, unused = lax.scan(
        scatter_group, start_grid, (grouped_deposit, grouped_cells, grouped_tiles)
    )
    partial_grid = accumulated.reshape(4, PX, PLANE)
    share_width = PLANE // deal_count
    summed = lax.psum(partial_grid, "deal")
    settled = smooth_planes(grid_update(summed))
    own_share = lax.dynamic_slice_in_dim(settled, deal_index * share_width, share_width, 2)
    tiles_view = settled.reshape(3, tile_count, TILE)

    def gather_group(pieces):
        part_cells, part_tiles = pieces
        selector = (part_cells[:, :, None] == tile_slots).astype(jnp.float32)
        chosen = jnp.take(tiles_view, part_tiles, axis=1)
        return jnp.einsum("cbk,bpk->bcp", chosen, selector, precision=highest)

    moved = lax.map(gather_group, (grouped_cells, grouped_tiles)).reshape(blocks_here, 3, 128)
    state = new_state(offsets, moved)
    records = jnp.concatenate([state, particle_mass[:, None, :]], axis=1)
    lists_here = send_lists[0, 0]
    counts_here = send_counts[0, 0]
    mig_slots = lists_here.shape[1]
    leaving = records[lists_here]
    keeping = (jnp.arange(mig_slots, dtype=jnp.int32)[None, :] < counts_here[:, None]).astype(
        jnp.float32
    )
    leaving = leaving * keeping[:, :, None, None]
    from_left = from_behind(leaving[0], "slab", 1)
    from_right = from_behind(leaving[1], "slab", -1)
    arrivals = jnp.stack([from_left, from_right], axis=0)[None, None]
    return (state, arrivals, own_share)


def solution(mesh):
    placed = (
        P(("slab", "deal"), None, None),
        P(("slab", "deal"), None, None),
        P(("slab", "deal"), None, None),
        P(("slab", "deal"), None),
        P(("slab", "deal"), None),
        P(("slab", "deal")),
        P("slab", "deal"),
        P("slab", "deal", None, None),
        P("slab", "deal", None),
    )
    return jax.shard_map(
        body,
        mesh=mesh,
        in_specs=placed,
        out_specs=(
            P(("slab", "deal"), None, None),
            P("slab", "deal", None, None, None, None),
            P(None, "slab", "deal"),
        ),
        check_vma=False,
    )
```

profile of v0, /device:TPU:36, one launch (start us, length us, event | category | flops | bytes accessed | tf_op | source)
XLA Modules:
  0.0 715.3 jit_solution(17750326959352518418)
XLA Ops:
  9.4 2.9 multiply_subtract_fusion.2
  14.9 2.3 pad_maximum_fusion.7
  17.1 127.7 %while.23 = (s32[]{:T(128)}, f32[4,2048,256]{1,2,0:T(8,128)}, f32[8,128,4,128]{3,2,1,0:T(4,128)}, s32[8,128,128]{2,1,0:T(8,128)}, s32[8,128]{1,0:T(8,128)}, /*index=5*/s32[]{:T(128)}, s32[]{:T(128)}) while((s32[]{:T(128)}, f32[4,2048,256]{1,2,0:T(8,128)}, f32[8,128,4,128]{3,2,1,0:T(4,128)}, s32[8,128,128]{2,1,0:T(8,128)}, ...), condition=%wide.region_1.2_spmd.clone, body=%wide.region_0.1_spmd.clone.sunk | while | flops 3431202816 | bytes 18286184 | solution.py:105
  18.7 6.5 fusion.76
  25.1 6.1 bitcast_add_fusion.2
  32.7 6.5 fusion.76
  39.2 8.2 %bitcast_add_fusion.2 = f32[4,2048,256]{1,2,0:T(8,128)} fusion(f32[4,2048,256]{1,2,0:T(8,128)} %get-tuple-element.245, pred[]{:T(512)S(6)} %compare.3, f32[128,4,256]{2,1,0:T(4,128)S(1)} %fusion.76, s32[128]{0:T(128)S(1)} %fusion.77), kind=kOutput, calls=%fused_computation.24.clone.1 | convolution fusion | flops 3225681920 | bytes 17302016 | tf_op jit(solution)/shard_map/while/body/eval_jaxpr/bt,bck->ctk/dot_general | solution.py:100
  49.0 6.5 fusion.76
  55.5 8.2 %bitcast_add_fusion.2 = f32[4,2048,256]{1,2,0:T(8,128)} fusion(f32[4,2048,256]{1,2,0:T(8,128)} %get-tuple-element.245, pred[]{:T(512)S(6)} %compare.3, f32[128,4,256]{2,1,0:T(4,128)S(1)} %fusion.76, s32[128]{0:T(128)S(1)} %fusion.77), kind=kOutput, calls=%fused_computation.24.clone.1 | convolution fusion | flops 3225681920 | bytes 17302016 | tf_op jit(solution)/shard_map/while/body/eval_jaxpr/bt,bck->ctk/dot_general | solution.py:100
  65.2 6.5 fusion.76
  71.7 8.2 %bitcast_add_fusion.2 = f32[4,2048,256]{1,2,0:T(8,128)} fusion(f32[4,2048,256]{1,2,0:T(8,128)} %get-tuple-element.245, pred[]{:T(512)S(6)} %compare.3, f32[128,4,256]{2,1,0:T(4,128)S(1)} %fusion.76, s32[128]{0:T(128)S(1)} %fusion.77), kind=kOutput, calls=%fused_computation.24.clone.1 | convolution fusion | flops 3225681920 | bytes 17302016 | tf_op jit(solution)/shard_map/while/body/eval_jaxpr/bt,bck->ctk/dot_general | solution.py:100
  81.5 6.5 fusion.76
  87.9 8.2 %bitcast_add_fusion.2 = f32[4,2048,256]{1,2,0:T(8,128)} fusion(f32[4,2048,256]{1,2,0:T(8,128)} %get-tuple-element.245, pred[]{:T(512)S(6)} %compare.3, f32[128,4,256]{2,1,0:T(4,128)S(1)} %fusion.76, s32[128]{0:T(128)S(1)} %fusion.77), kind=kOutput, calls=%fused_computation.24.clone.1 | convolution fusion | flops 3225681920 | bytes 17302016 | tf_op jit(solution)/shard_map/while/body/eval_jaxpr/bt,bck->ctk/dot_general | solution.py:100
  97.7 6.5 fusion.76
  104.2 8.2 %bitcast_add_fusion.2 = f32[4,2048,256]{1,2,0:T(8,128)} fusion(f32[4,2048,256]{1,2,0:T(8,128)} %get-tuple-element.245, pred[]{:T(512)S(6)} %compare.3, f32[128,4,256]{2,1,0:T(4,128)S(1)} %fusion.76, s32[128]{0:T(128)S(1)} %fusion.77), kind=kOutput, calls=%fused_computation.24.clone.1 | convolution fusion | flops 3225681920 | bytes 17302016 | tf_op jit(solution)/shard_map/while/body/eval_jaxpr/bt,bck->ctk/dot_general | solution.py:100
  113.9 6.5 fusion.76
  120.4 8.2 %bitcast_add_fusion.2 = f32[4,2048,256]{1,2,0:T(8,128)} fusion(f32[4,2048,256]{1,2,0:T(8,128)} %get-tuple-element.245, pred[]{:T(512)S(6)} %compare.3, f32[128,4,256]{2,1,0:T(4,128)S(1)} %fusion.76, s32[128]{0:T(128)S(1)} %fusion.77), kind=kOutput, calls=%fused_computation.24.clone.1 | convolution fusion | flops 3225681920 | bytes 17302016 | tf_op jit(solution)/shard_map/while/body/eval_jaxpr/bt,bck->ctk/dot_general | solution.py:100
  130.2 6.5 fusion.76
  136.7 8.2 %bitcast_add_fusion.2 = f32[4,2048,256]{1,2,0:T(8,128)} fusion(f32[4,2048,256]{1,2,0:T(8,128)} %get-tuple-element.245, pred[]{:T(512)S(6)} %compare.3, f32[128,4,256]{2,1,0:T(4,128)S(1)} %fusion.76, s32[128]{0:T(128)S(1)} %fusion.77), kind=kOutput, calls=%fused_computation.24.clone.1 | convolution fusion | flops 3225681920 | bytes 17302016 | tf_op jit(solution)/shard_map/while/body/eval_jaxpr/bt,bck->ctk/dot_general | solution.py:100
  144.9 8.7 %copy.94 = f32[4,2048,256]{2,1,0:T(8,128)} copy(f32[4,2048,256]{1,2,0:T(8,128)} %get-tuple-element.72) | data formatting | bytes 16777216 | tf_op jit(solution)/shard_map/while | solution.py:105
  153.6 9.4 %reshape.134 = f32[4,64,8192]{2,1,0:T(8,128)} reshape(f32[4,2048,256]{2,1,0:T(8,128)} %copy.94) | data formatting | bytes 16777216 | tf_op jit(solution)/shard_map/reshape | solution.py:108
  163.8 344.7 %all-reduce.2.cloned.1.call-done = f32[4,64,8192]{2,1,0:T(8,128)} async-done(((f32[4,64,8192]{2,1,0:T(8,128)}), f32[4,64,8192]{2,1,0:T(8,128)}) %all-reduce.2.cloned.1.call-update) | async-done | bytes 8388624 | tf_op jit(solution)/shard_map/psum | solution.py:110
  508.5 4.3 fusion.30
  515.7 6.2 collective-permute-start
  524.4 4.4 fusion.28
  528.8 7.1 reshape.135
  535.8 10.7 %copy.99 = f32[3,2048,256]{2,0,1:T(4,128)} copy(f32[3,2048,256]{2,1,0:T(8,128)} %reshape.135) | data formatting | bytes 12582912
  546.5 130.2 %while.22 = (s32[]{:T(128)}, f32[8,128,3,128]{3,1,0,2:T(8,128)S(1)}, s32[8,128]{1,0:T(8,128)}, f32[3,2048,256]{2,0,1:T(4,128)}, s32[8,128,128]{2,1,0:T(8,128)}, /*index=5*/s32[]{:T(128)}) while((s32[]{:T(128)}, f32[8,128,3,128]{3,1,0,2:T(8,128)S(1)}, s32[8,128]{1,0:T(8,128)}, f32[3,2048,256]{2,0,1:T(4,128)}, ...), condition=%wide.region_4.5_spmd.clone, body=%wide.region_3.4_spmd.clone.sunk | while | flops 155289728 | bytes 2038621 | solution.py:121
  548.9 5.0 gather_fusion
  553.9 8.9 %fusion.72 = f32[1,128,3,128]{3,2,1,0:T(4,128)S(1)} fusion(s32[128,128]{1,0:T(8,128)S(1)} %dynamic-slice_bitcast_fusion.4, f32[128,3,256]{2,1,0:T(4,128)} %gather_fusion, pred[128]{0:T(512)(128)(4,1)S(1)} %compare_and_fusion.2), kind=kOutput, calls=%fused_computation.8.clone.1 | convolution fusion | flops 155287552 | bytes 655488 | tf_op jit(solution)/shard_map/while/body/eval_jaxpr/cbk,bpk->bcp/dot_general | solution.py:119
  565.2 5.0 gather_fusion
  570.2 8.9 %fusion.72 = f32[1,128,3,128]{3,2,1,0:T(4,128)S(1)} fusion(s32[128,128]{1,0:T(8,128)S(1)} %dynamic-slice_bitcast_fusion.4, f32[128,3,256]{2,1,0:T(4,128)} %gather_fusion, pred[128]{0:T(512)(128)(4,1)S(1)} %compare_and_fusion.2), kind=kOutput, calls=%fused_computation.8.clone.1 | convolution fusion | flops 155287552 | bytes 655488 | tf_op jit(solution)/shard_map/while/body/eval_jaxpr/cbk,bpk->bcp/dot_general | solution.py:119
  581.4 5.0 gather_fusion
  586.5 8.9 %fusion.72 = f32[1,128,3,128]{3,2,1,0:T(4,128)S(1)} fusion(s32[128,128]{1,0:T(8,128)S(1)} %dynamic-slice_bitcast_fusion.4, f32[128,3,256]{2,1,0:T(4,128)} %gather_fusion, pred[128]{0:T(512)(128)(4,1)S(1)} %compare_and_fusion.2), kind=kOutput, calls=%fused_computation.8.clone.1 | convolution fusion | flops 155287552 | bytes 655488 | tf_op jit(solution)/shard_map/while/body/eval_jaxpr/cbk,bpk->bcp/dot_general | solution.py:119
  597.7 5.0 gather_fusion
  602.7 8.9 %fusion.72 = f32[1,128,3,128]{3,2,1,0:T(4,128)S(1)} fusion(s32[128,128]{1,0:T(8,128)S(1)} %dynamic-slice_bitcast_fusion.4, f32[128,3,256]{2,1,0:T(4,128)} %gather_fusion, pred[128]{0:T(512)(128)(4,1)S(1)} %compare_and_fusion.2), kind=kOutput, calls=%fused_computation.8.clone.1 | convolution fusion | flops 155287552 | bytes 655488 | tf_op jit(solution)/shard_map/while/body/eval_jaxpr/cbk,bpk->bcp/dot_general | solution.py:119
  613.9 5.0 gather_fusion
  619.0 8.9 %fusion.72 = f32[1,128,3,128]{3,2,1,0:T(4,128)S(1)} fusion(s32[128,128]{1,0:T(8,128)S(1)} %dynamic-slice_bitcast_fusion.4, f32[128,3,256]{2,1,0:T(4,128)} %gather_fusion, pred[128]{0:T(512)(128)(4,1)S(1)} %compare_and_fusion.2), kind=kOutput, calls=%fused_computation.8.clone.1 | convolution fusion | flops 155287552 | bytes 655488 | tf_op jit(solution)/shard_map/while/body/eval_jaxpr/cbk,bpk->bcp/dot_general | solution.py:119
  630.2 5.0 gather_fusion
  635.2 8.9 %fusion.72 = f32[1,128,3,128]{3,2,1,0:T(4,128)S(1)} fusion(s32[128,128]{1,0:T(8,128)S(1)} %dynamic-slice_bitcast_fusion.4, f32[128,3,256]{2,1,0:T(4,128)} %gather_fusion, pred[128]{0:T(512)(128)(4,1)S(1)} %compare_and_fusion.2), kind=kOutput, calls=%fused_computation.8.clone.1 | convolution fusion | flops 155287552 | bytes 655488 | tf_op jit(solution)/shard_map/while/body/eval_jaxpr/cbk,bpk->bcp/dot_general | solution.py:119
  646.5 5.0 gather_fusion
  651.5 8.9 %fusion.72 = f32[1,128,3,128]{3,2,1,0:T(4,128)S(1)} fusion(s32[128,128]{1,0:T(8,128)S(1)} %dynamic-slice_bitcast_fusion.4, f32[128,3,256]{2,1,0:T(4,128)} %gather_fusion, pred[128]{0:T(512)(128)(4,1)S(1)} %compare_and_fusion.2), kind=kOutput, calls=%fused_computation.8.clone.1 | convolution fusion | flops 155287552 | bytes 655488 | tf_op jit(solution)/shard_map/while/body/eval_jaxpr/cbk,bpk->bcp/dot_general | solution.py:119
  662.7 5.0 gather_fusion
  667.8 8.9 %fusion.72 = f32[1,128,3,128]{3,2,1,0:T(4,128)S(1)} fusion(s32[128,128]{1,0:T(8,128)S(1)} %dynamic-slice_bitcast_fusion.4, f32[128,3,256]{2,1,0:T(4,128)} %gather_fusion, pred[128]{0:T(512)(128)(4,1)S(1)} %compare_and_fusion.2), kind=kOutput, calls=%fused_computation.8.clone.1 | convolution fusion | flops 155287552 | bytes 655488 | tf_op jit(solution)/shard_map/while/body/eval_jaxpr/cbk,bpk->bcp/dot_general | solution.py:119
  678.7 3.2 copy-done.3
  681.9 8.1 %copy.101 = f32[1024,16,128]{2,1,0:T(8,128)} copy(f32[1024,16,128]{2,0,1:T(8,128)S(1)} %get-tuple-element.173) | data formatting | bytes 16777216 | tf_op jit(solution)/shard_map/concatenate | solution.py:123
  690.0 3.9 gather_fusion.1
  696.0 6.2 collective-permute-start.3
  (111 shorter events, 50.9 us)
Async XLA Ops:
  7.2 5.8 copy-start.1
  7.2 501.4 %all-reduce.2.cloned.1.call-start = ((), (), s32[]{:S(2)}) async-start(), calls=%async_computation | async-start | bytes 16777216 | tf_op jit(solution)/shard_map/psum | solution.py:110
  163.0 0.7 copy-start.4
  163.0 0.8 copy-start.5
  513.8 9.2 %collective-permute-start.1 = (f32[3,1,8192]{2,0,1:T(4,128)S(1)}, f32[3,1,8192]{2,0,1:T(4,128)S(1)}, u32[]{:S(2)}, u32[]{:S(2)}) collective-permute-start(f32[3,1,8192]{2,0,1:T(4,128)S(1)} %copy.97), channel_id=1, source_target_pairs={{0,8},{8,16},{16,24},{24,32},{32,40},{40,48},{48,56},{56,64},{64,7... | collective-permute-start | bytes 294920 | tf_op jit(solution)/shard_map/ppermute | solution.py:22
  515.7 8.6 %collective-permute-start = (f32[3,1,8192]{2,0,1:T(4,128)S(1)}, f32[3,1,8192]{2,0,1:T(4,128)S(1)}, u32[]{:S(2)}, u32[]{:S(2)}) collective-permute-start(f32[3,1,8192]{2,0,1:T(4,128)S(1)} %copy.95), channel_id=1, source_target_pairs={{8,0},{16,8},{24,16},{32,24},{40,32},{48,40},{56,48},{64,56},{72,6... | collective-permute-start | bytes 294920 | tf_op jit(solution)/shard_map/ppermute | solution.py:23
  546.5 130.2 %copy-start = (f32[1024,3,128]{2,0,1:T(8,128)S(1)}, f32[1024,3,128]{2,0,1:T(8,128)}, u32[]{:S(2)}) copy-start(f32[1024,3,128]{2,0,1:T(8,128)} %param.13) | copy-start | bytes 4718596
  677.5 1.0 copy-start.2
  678.7 3.2 copy-start.3
  694.1 13.6 %collective-permute-start.2 = (f32[16,16,128]{2,1,0:T(8,128)S(1)}, f32[16,16,128]{2,1,0:T(8,128)S(1)}, u32[]{:S(2)}, u32[]{:S(2)}) collective-permute-start(f32[16,16,128]{2,1,0:T(8,128)S(1)} %get-tuple-element.171), channel_id=1, source_target_pairs={{0,8},{8,16},{16,24},{24,32},{32,40},{40,48},{48,56},{56,64},{64,7... | collective-permute-start | bytes 393224 | tf_op jit(solution)/shard_map/ppermute | solution.py:31
  696.0 11.7 %collective-permute-start.3 = (f32[16,16,128]{2,1,0:T(8,128)S(1)}, f32[16,16,128]{2,1,0:T(8,128)S(1)}, u32[]{:S(2)}, u32[]{:S(2)}) collective-permute-start(f32[16,16,128]{2,1,0:T(8,128)S(1)} %get-tuple-element.172), channel_id=1, source_target_pairs={{8,0},{16,8},{24,16},{32,24},{40,32},{48,40},{56,48},{64,56},{72,6... | collective-permute-start | bytes 393224 | tf_op jit(solution)/shard_map/ppermute | solution.py:31
Sparse Core Ops, SparseCore 0:
  163.1 345.3 all-reduce.1
where the time goes:
time: 718 us; the launch traced here: 715 us
  waiting for transfers between devices  347 us (48%)
  matrix products  187 us (26%)
  local copies, waits for them, and re-layouts  115 us (16%)
  other arithmetic  35.2 us (5%)
  starting transfers between devices  16.3 us (2%)
  between operations  15 us (2%)
    psum x1, waiting for transfers between devices, body(): summed = lax.psum(partial_grid, 'deal')  345 us
    dot_general x8, matrix products, gather_group(): return jnp.einsum('cbk,bpk->bcp', chosen, selector, precision=highest)  71.3 us
    dot_general x8, matrix products, scatter_group(): jnp.einsum('bt,bck->ctk', placing, per_block, precision=highest)  63.6 us
    dot_general x8, matrix products, scatter_group(): jnp.einsum('bcp,bpk->bck', part_deposit, selector, precision=highest)  51.9 us
    gather x8, local copies, waits for them, and re-layouts, gather_group(): chosen = jnp.take(tiles_view, part_tiles, axis=1)  40.3 us
    unnamed x14, local copies, waits for them, and re-layouts  15.4 us
  transfers between devices with their start and end apart: 5, of which 3 were waited for; matrix products, arithmetic and copies ran while one was open for 1% of the time, Pallas kernels for 0%

commit v1 on v0

--- a/solution.py
+++ b/solution.py
@@ -107,7 +107,7 @@
     )
     partial_grid = accumulated.reshape(4, PX, PLANE)
     share_width = PLANE // deal_count
-    summed = lax.psum(partial_grid, "deal")
+    summed = jnp.sum(lax.all_gather(partial_grid, "deal"), axis=0)
     settled = smooth_planes(grid_update(summed))
     own_share = lax.dynamic_slice_in_dim(settled, deal_index * share_width, share_width, 2)
     tiles_view = settled.reshape(3, tile_count, TILE)

time: 718 us -> 1670 us (2.33)
  waiting for transfers between devices: 347 us -> 1280 us
  other arithmetic: 35.2 us -> 60.9 us
    all_gather x0 -> x1, waiting for transfers between devices: none -> 1270 us  [body(): summed = jnp.sum(lax.all_gather(partial_grid, 'deal'), axis=0)]
    psum x1 -> x0, waiting for transfers between devices: 345 us -> none  [body(): summed = lax.psum(partial_grid, 'deal')]
    reduce_sum x0 -> x1, other arithmetic: none -> 24.4 us  [body(): summed = jnp.sum(lax.all_gather(partial_grid, 'deal'), axis=0)]
  transfers between devices with their start and end apart: 5 -> 5, of which waited for: 3 -> 3; matrix products, arithmetic and copies ran while one was open for 1% -> 0% of each run, Pallas kernels for 0% -> 0%
where the time goes in v1:
time: 1670 us
  waiting for transfers between devices  1280 us (77%)
  matrix products  187 us (11%)
  local copies, waits for them, and re-layouts  115 us (7%)
  other arithmetic  60.9 us (4%)
    all_gather x1, waiting for transfers between devices, body(): summed = jnp.sum(lax.all_gather(partial_grid, 'deal'), axis=0)  1270 us
    dot_general x8, matrix products, gather_group(): return jnp.einsum('cbk,bpk->bcp', chosen, selector, precision=highest)  71.3 us
    dot_general x8, matrix products, scatter_group(): jnp.einsum('bt,bck->ctk', placing, per_block, precision=highest)  63.8 us
    dot_general x8, matrix products, scatter_group(): jnp.einsum('bcp,bpk->bck', part_deposit, selector, precision=highest)  51.9 us
    gather x8, local copies, waits for them, and re-layouts, gather_group(): chosen = jnp.take(tiles_view, part_tiles, axis=1)  40.3 us
  transfers between devices with their start and end apart: 5, of which 3 were waited for; matrix products, arithmetic and copies ran while one was open for 0% of the time, Pallas kernels for 0%

profile of v1, /device:TPU:36, one launch (start us, length us, event | category | flops | bytes accessed | tf_op | source)
XLA Modules:
  0.0 1669.5 jit_solution(1526120779859189258)
XLA Ops:
  18.6 128.0 %while.23 = (s32[]{:T(128)}, f32[4,2048,256]{1,2,0:T(8,128)}, f32[8,128,4,128]{3,2,1,0:T(4,128)}, s32[8,128,128]{2,1,0:T(8,128)}, s32[8,128]{1,0:T(8,128)}, /*index=5*/s32[]{:T(128)}, s32[]{:T(128)}) while((s32[]{:T(128)}, f32[4,2048,256]{1,2,0:T(8,128)}, f32[8,128,4,128]{3,2,1,0:T(4,128)}, s32[8,128,128]{2,1,0:T(8,128)}, ...), condition=%wide.region_1.2_spmd.clone, body=%wide.region_0.1_spmd.clone.sunk | while | flops 3431202816 | bytes 18286684 | solution.py:105
  19.5 6.5 fusion.76
  26.6 6.1 bitcast_add_fusion.2
  33.6 6.5 fusion.76
  40.7 8.2 bitcast_add_fusion.2
  49.8 6.5 fusion.76
  57.0 8.2 bitcast_add_fusion.2
  66.1 6.5 fusion.76
  73.3 8.3 bitcast_add_fusion.2
  82.4 6.5 fusion.76
  89.6 8.2 bitcast_add_fusion.2
  98.7 6.5 fusion.76
  105.9 8.2 bitcast_add_fusion.2
  114.9 6.5 fusion.76
  122.1 8.2 bitcast_add_fusion.2
  131.2 6.5 fusion.76
  138.4 8.2 bitcast_add_fusion.2
  146.7 8.7 copy.94
  155.4 9.4 all_gather_reshape.3
  165.6 1270.7 %all-gather.2.cloned.1.call-done = f32[8,4,64,8192]{3,2,1,0:T(8,128)} async-done(((f32[1,4,64,8192]{3,2,1,0:T(8,128)}), f32[8,4,64,8192]{3,2,1,0:T(8,128)}) %all-gather.2.cloned.1.call-update) | async-done | bytes 67108880 | tf_op jit(solution)/shard_map/all_gather | solution.py:110
  1436.3 24.4 %reduce_sum.9 = f32[4,64,8192]{2,1,0:T(8,128)} reduce(f32[8,4,64,8192]{3,2,1,0:T(8,128)} %all-gather.2.cloned.1.call-done, f32[]{:T(128)} %constant.31.clone.1), dimensions={0}, to_apply=%region_2.3 | reduce | flops 14680064 | bytes 75497472 | tf_op jit(solution)/shard_map/reduce_sum | solution.py:110
  1460.7 4.3 fusion.30
  1465.9 4.1 collective-permute-start
  1472.6 6.2 collective-permute-done.1
  1478.9 4.4 fusion.28
  1483.3 7.1 reshape.131
  1490.4 10.7 copy.99
  1501.1 130.0 %while.22 = (s32[]{:T(128)}, f32[8,128,3,128]{3,1,0,2:T(8,128)S(1)}, s32[8,128]{1,0:T(8,128)}, f32[3,2048,256]{2,0,1:T(4,128)}, s32[8,128,128]{2,1,0:T(8,128)}, /*index=5*/s32[]{:T(128)}) while((s32[]{:T(128)}, f32[8,128,3,128]{3,1,0,2:T(8,128)S(1)}, s32[8,128]{1,0:T(8,128)}, f32[3,2048,256]{2,0,1:T(4,128)}, ...), condition=%wide.region_4.5_spmd.clone, body=%wide.region_3.4_spmd.clone.sunk | while | flops 155289728 | bytes 2038613 | solution.py:121
  1501.8 5.0 gather_fusion
  1508.3 8.9 fusion.72
  1518.0 5.0 gather_fusion
  1524.6 8.9 fusion.72
  1534.3 5.0 gather_fusion
  1540.9 8.9 fusion.72
  1550.5 5.0 gather_fusion
  1557.1 8.9 fusion.72
  1566.8 5.0 gather_fusion
  1573.4 8.9 fusion.72
  1583.0 5.0 gather_fusion
  1589.6 8.9 fusion.72
  1599.3 5.0 gather_fusion
  1605.9 8.9 fusion.72
  1615.6 5.0 gather_fusion
  1622.1 8.9 fusion.72
  1633.0 3.2 copy-done.3
  1636.3 8.1 copy.101
  1644.4 3.9 gather_fusion.1
  1650.4 6.0 collective-permute-start.3
  (112 shorter events, 55.7 us)
Async XLA Ops:
  7.2 3.1 copy-start
  7.2 6.3 copy-start.1
  7.2 1429.1 %all-gather.2.cloned.1.call-start = ((), (), s32[]{:S(2)}) async-start(), calls=%async_computation | async-start | bytes 75497472 | tf_op jit(solution)/shard_map/all_gather | solution.py:110
  164.8 0.7 copy-start.4
  164.8 0.8 copy-start.5
  1465.9 6.7 collective-permute-start
  1470.1 8.7 collective-permute-start.1
  1631.8 1.0 copy-start.2
  1633.0 3.2 copy-start.3
  1648.4 13.5 collective-permute-start.2
  1650.4 11.5 collective-permute-start.3
Sparse Core Ops, SparseCore 0:
  164.9 1271.3 all-gather.1
